TPU v7x, 512 devices: a whole 4x4x16 slice. The times are simulated.
512 devices in a mesh: ctx: 64 (over z, x_hi, core), head: 8 (over x_lo, y).
Axes of the slice: x: 4 (x_hi: 2, x_lo: 2; x = x_hi * 2 + x_lo), y: 4, z: 16, core: 2. Of those that a mesh axis runs over, the one named last changes fastest.
Arguments:
- queries: bfloat16 [16384, 4096], P('ctx', 'head'), may hold values from -6 to 6
- key_rows: bfloat16 [16384, 1024], P('ctx', 'head'), may hold values from -6 to 6
- value_rows: bfloat16 [16384, 1024], P('ctx', 'head'), may hold values from -6 to 6
- attn_out: bfloat16 [16384, 4096], P('ctx', 'head'), may hold values from -6 to 6
- out_grad: bfloat16 [16384, 4096], P('ctx', 'head'), may hold values from -6 to 6
- log_sums: float32 [32, 16384], P('head', 'ctx'), may hold values from 4.5 to 6
- block_picks: int32 [128, 32, 3], P('ctx', 'head'), may hold values from 0 to 3, all different within a row
- query_weight: bfloat16 [4096, 4096], P('ctx', 'head'), may hold values from -0.21875 to 0.21875
- key_weight: bfloat16 [4096, 1024], P('ctx', 'head'), may hold values from -0.21875 to 0.21875
- value_weight: bfloat16 [4096, 1024], P('ctx', 'head'), may hold values from -0.21875 to 0.21875
Outputs:
- input_grad: bfloat16 [16384, 4096], P('ctx', 'head')
Inputs may be any that keep to these rules, and one draw needn't show every extreme that they name: `block_picks`: in each row (query block, query head) the 3 entries differ; entry m selects the block m + 1 blocks before the query's block, and selections before the sequence's start select nothing.
All inputs are finite; a program needn't handle non-finite values.
Results may differ from a plain program's by a relative error of at most 0.013.
Values may be sent and summed in bfloat16 or wider, within the bound.
No kernel may reach another device: no remote copies, remote signals or barrier semaphores. Data moves between devices by JAX's collectives and lax.ppermute only.
A program may use at most 64 MiB of HBM per device.

v0:
```python
import math
import jax
import jax.numpy as jnp
from jax import lax
from jax.sharding import PartitionSpec as P

BLK = 128


def passed_along(x, axis, by):
    devices = lax.axis_size(axis)
    pairs = [(i, i + by) for i in range(devices) if 0 <= i + by < devices]
    return lax.ppermute(x, axis, pairs)


def block_grads(
    query_blocks,
    grad_blocks,
    log_part,
    delta_part,
    pick_part,
    query_first,
    key_table,
    value_table,
    key_first,
):
    blocks, width, group, head_dim = query_blocks.shape
    table_blocks = key_table.shape[0]
    scaling = 1.0 / math.sqrt(head_dim)
    offsets = jnp.concatenate([jnp.zeros((blocks, group, 1), jnp.int32), pick_part + 1], axis=2)
    query_ids = query_first + jnp.arange(blocks, dtype=jnp.int32)
    key_block = query_ids[:, None, None] - offsets
    table_index = key_block - key_first
    usable = (table_index >= 0) & (table_index < table_blocks) & (key_block >= 0)
    clipped = jnp.clip(table_index, 0, table_blocks - 1)
    key_sel = key_table[clipped]
    value_sel = value_table[clipped]
    scores = (
        jnp.einsum("bqgd,bgskd->bgqsk", query_blocks, key_sel, preferred_element_type=jnp.float32)
        * scaling
    )
    position = jnp.arange(width)
    causal = position[:, None] >= position[None, :]
    allowed = usable[:, :, None, :, None] & (
        (offsets != 0)[:, :, None, :, None] | causal[None, None, :, None, :]
    )
    probability = jnp.where(allowed, jnp.exp(scores - log_part[:, :, :, None, None]), 0.0)
    prob_grad = jnp.einsum(
        "bqgd,bgskd->bgqsk", grad_blocks, value_sel, preferred_element_type=jnp.float32
    )
    score_grad = probability * (prob_grad - delta_part[:, :, :, None, None])
    prob_half = probability.astype(jnp.bfloat16)
    grad_half = score_grad.astype(jnp.bfloat16)
    query_grad = (
        jnp.einsum("bgqsk,bgskd->bqgd", grad_half, key_sel, preferred_element_type=jnp.float32)
        * scaling
    )
    key_terms = (
        jnp.einsum("bgqsk,bqgd->bgskd", grad_half, query_blocks, preferred_element_type=jnp.float32)
        * scaling
    )
    value_terms = jnp.einsum(
        "bgqsk,bqgd->bgskd", prob_half, grad_blocks, preferred_element_type=jnp.float32
    )
    onehot = (usable[..., None] & (clipped[..., None] == jnp.arange(table_blocks))).astype(
        jnp.float32
    )
    key_grad = jnp.einsum("bgsc,bgskd->ckd", onehot, key_terms, precision=lax.Precision.HIGHEST)
    value_grad = jnp.einsum("bgsc,bgskd->ckd", onehot, value_terms, precision=lax.Precision.HIGHEST)
    return (query_grad, key_grad, value_grad)


def per_device(
    queries,
    key_rows,
    value_rows,
    attn_out,
    out_grad,
    log_sums,
    block_picks,
    query_weight,
    key_weight,
    value_weight,
):
    tokens, query_cols = queries.shape
    head_dim = key_rows.shape[1]
    group = query_cols // head_dim
    width = BLK
    blocks = tokens // width
    cycle_pos = lax.axis_index("ctx")
    own_first = cycle_pos * blocks
    query_blocks = queries.reshape(blocks, width, group, head_dim)
    grad_blocks = out_grad.reshape(blocks, width, group, head_dim)
    delta_part = jnp.sum(
        (out_grad.astype(jnp.float32) * attn_out.astype(jnp.float32)).reshape(
            blocks, width, group, head_dim
        ),
        axis=3,
    ).transpose(0, 2, 1)
    log_part = log_sums.reshape(group, blocks, width).transpose(1, 0, 2)
    fetched = []
    for distance in (1, 2):
        fetched.append(passed_along((key_rows, value_rows), "ctx", distance))
    key_table = jnp.concatenate([fetched[1][0], fetched[0][0], key_rows], axis=0).reshape(
        3 * blocks, width, head_dim
    )
    value_table = jnp.concatenate([fetched[1][1], fetched[0][1], value_rows], axis=0).reshape(
        3 * blocks, width, head_dim
    )
    query_grad, key_grad, value_grad = block_grads(
        query_blocks,
        grad_blocks,
        log_part,
        delta_part,
        block_picks,
        own_first,
        key_table,
        value_table,
        own_first - 2 * blocks,
    )
    key_own = key_grad[2 * blocks :]
    value_own = value_grad[2 * blocks :]
    for distance in (1, 2):
        lower = (2 - distance) * blocks
        returned = passed_along(
            (key_grad[lower : lower + blocks], value_grad[lower : lower + blocks]), "ctx", -distance
        )
        key_own = key_own + returned[0]
        value_own = value_own + returned[1]
    grads = jnp.concatenate(
        [
            query_grad.reshape(tokens, query_cols).astype(jnp.bfloat16),
            key_own.reshape(tokens, head_dim).astype(jnp.bfloat16),
            value_own.reshape(tokens, head_dim).astype(jnp.bfloat16),
        ],
        axis=1,
    )
    weight_cat = jnp.concatenate([query_weight, key_weight, value_weight], axis=1)
    partial_value = lax.dot_general(
        grads,
        lax.all_gather(weight_cat, "ctx", axis=0, tiled=True),
        (((1,), (1,)), ((), ())),
        preferred_element_type=jnp.float32,
    )
    return lax.psum_scatter(
        partial_value.astype(jnp.bfloat16), "head", scatter_dimension=1, tiled=True
    )


def solution(mesh):
    placed = (
        P("ctx", "head"),
        P("ctx", "head"),
        P("ctx", "head"),
        P("ctx", "head"),
        P("ctx", "head"),
        P("head", "ctx"),
        P("ctx", "head", None),
        P("ctx", "head"),
        P("ctx", "head"),
        P("ctx", "head"),
    )
    return jax.shard_map(
        per_device, mesh=mesh, in_specs=placed, out_specs=P("ctx", "head"), check_vma=False
    )
```

profile of v0, /device:TPU:4, one launch (start us, length us, event | category | flops | bytes accessed | tf_op | source)
XLA Modules:
  0.0 230.7 jit_solution(6480486702893773419)
XLA Ops:
  6.5 1.5 pad_maximum_fusion.2
  8.1 0.0 all-gather.2.cloned.1.call-update
  8.1 0.0 reduce-scatter.2.cloned.1.call-start
  8.1 3.8 %collective-permute-start = (bf16[256,128]{1,0:T(8,128)(2,1)}, bf16[256,128]{1,0:T(8,128)(2,1)S(1)}, u32[]{:S(2)}, u32[]{:S(2)}) collective-permute-start(bf16[256,128]{1,0:T(8,128)(2,1)} %param.11), channel_id=1, source_target_pairs={{0,16},{8,24},{16,32},{24,40},{32,48},{40,56},{48,64},{56,72},{64,... | collective-permute-start | bytes 196616 | tf_op jit(solution)/shard_map/ppermute | solution.py:13
  11.9 1.9 collective-permute-start.1
  13.8 4.9 %collective-permute-start.2 = (bf16[256,128]{1,0:T(8,128)(2,1)}, bf16[256,128]{1,0:T(8,128)(2,1)S(1)}, u32[]{:S(2)}, u32[]{:S(2)}) collective-permute-start(bf16[256,128]{1,0:T(8,128)(2,1)} %param.12), channel_id=1, source_target_pairs={{0,16},{8,24},{16,32},{24,40},{32,48},{40,56},{48,64},{56,72},{64,... | collective-permute-start | bytes 196616 | tf_op jit(solution)/shard_map/ppermute | solution.py:13
  18.8 3.6 %collective-permute-start.3 = (bf16[256,128]{1,0:T(8,128)(2,1)}, bf16[256,128]{1,0:T(8,128)(2,1)S(1)}, u32[]{:S(2)}, u32[]{:S(2)}) collective-permute-start(bf16[256,128]{1,0:T(8,128)(2,1)} %param.12), channel_id=1, source_target_pairs={{0,8},{8,16},{16,24},{24,32},{32,40},{40,48},{48,56},{56,64},{64,7... | collective-permute-start | bytes 196616 | tf_op jit(solution)/shard_map/ppermute | solution.py:13
  22.4 0.7 broadcast_add_fusion
  23.1 0.1 compare_select_fusion
  23.2 0.1 copy.38
  23.3 0.1 reshape.54
  23.4 0.1 compare_and_fusion
  23.4 0.1 copy.40
  23.6 0.1 copy.41
  23.7 1.0 reshape.47
  24.7 1.0 reshape.50
  25.7 1.1 convert_multiply_fusion
  26.8 0.0 copy-start.1
  26.8 0.2 reshape.51
  27.0 0.3 reduce_sum.9
  27.4 0.1 copy.46
  27.4 0.1 copy.50
  27.6 0.0 collective-permute-done.1
  27.6 0.0 copy-start.2
  27.7 0.7 gather_fusion
  28.5 0.7 gather_fusion.1
  29.2 0.7 bitcast_select_fusion
  30.0 0.5 fusion
  30.4 0.4 convolution_multiply_fusion
  30.9 3.3 %fusion.5 = f32[6,128,128]{2,0,1:T(8,128)S(1)} fusion(f32[2,4,4,128,128]{4,3,2,1,0:T(8,128)S(1)} %convolution_multiply_fusion, s32[2,4,4]{2,1,0:T(4,128)S(1)} %copy.50, pred[2,4,4]{2,1,0:T(4,128)(4,1)S(1)} %copy.40), kind=kOutput, calls=%fused_computation.11 | convolution fusion | flops 37749120 | bytes 2490528 | tf_op jit(solution)/shard_map/bgsc,bgskd->ckd/dot_general | solution.py:68
  34.2 0.1 fusion.34
  34.3 3.5 %collective-permute-start.4 = (f32[2,128,128]{2,0,1:T(2,128)S(1)}, f32[2,128,128]{2,0,1:T(2,128)S(1)}, u32[]{:S(2)}, u32[]{:S(2)}) collective-permute-start(f32[2,128,128]{2,0,1:T(2,128)S(1)} %get-tuple-element.7), channel_id=1, source_target_pairs={{8,0},{16,8},{24,16},{32,24},{40,32},{48,40},{56,48},{64,56},{72,6... | collective-permute-start | bytes 393224 | tf_op jit(solution)/shard_map/ppermute | solution.py:13
  37.8 1.9 collective-permute-start.5
  39.7 0.4 fusion.14
  40.1 3.3 %fusion.8 = f32[6,128,128]{2,0,1:T(8,128)S(1)} fusion(f32[2,4,4,128,128]{4,3,2,1,0:T(8,128)S(1)} %fusion.14, s32[2,4,4]{2,1,0:T(4,128)S(1)} %copy.50, pred[2,4,4]{2,1,0:T(4,128)(4,1)S(1)} %copy.40), kind=kOutput, calls=%fused_computation.12 | convolution fusion | flops 37749120 | bytes 2490528 | tf_op jit(solution)/shard_map/bgsc,bgskd->ckd/dot_general | solution.py:69
  43.4 0.5 fusion.13
  43.9 0.1 fusion.35
  44.0 1.9 collective-permute-start.6
  46.0 1.9 collective-permute-start.7
  47.9 0.2 copy.48
  48.2 0.1 fusion.28
  48.3 0.1 collective-permute-done.6
  48.5 8.6 %collective-permute-done.7 = f32[2,128,128]{2,0,1:T(2,128)S(1)} collective-permute-done((f32[2,128,128]{2,0,1:T(2,128)S(1)}, f32[2,128,128]{2,0,1:T(2,128)S(1)}, u32[]{:S(2)}, u32[]{:S(2)}) %collective-permute-start.7) | collective-permute-done | bytes 131104 | tf_op jit(solution)/shard_map/ppermute | solution.py:13
  57.1 0.1 fusion.26
  57.2 113.4 %all-gather.2.cloned.1.call-done = bf16[4096,768]{1,0:T(8,128)(2,1)} async-done(((bf16[64,768]{1,0:T(8,128)(2,1)}), bf16[4096,768]{1,0:T(8,128)(2,1)}) %all-gather.2.cloned.1.call-update) | async-done | bytes 6291472 | tf_op jit(solution)/shard_map/all_gather | solution.py:141
  170.6 6.0 %convolution_convert_fusion = bf16[256,4096]{1,0:T(8,128)(2,1)} fusion(bf16[4096,768]{1,0:T(8,128)(2,1)} %all-gather.2.cloned.1.call-done, bf16[256,128]{1,0:T(8,128)(2,1)S(1)} %bitcast.71, bf16[256,128]{1,0:T(8,128)(2,1)S(1)} %bitcast.70, bf16[256,512]{1,0:T(8,128)(2,1)S(1)} %bitcast.69), kind=kOutput, calls=%fused_computation.2 | convolution fusion | flops 1612840960 | bytes 8781824 | tf_op jit(solution)/shard_map/dot_general | solution.py:139
  176.6 0.0 reduce-scatter.2.cloned.1.call-update
  176.6 47.3 %reduce-scatter.2.cloned.1.call-done = bf16[256,512]{1,0:T(8,128)(2,1)} async-done(((bf16[256,4096]{1,0:T(8,128)(2,1)}), bf16[256,512]{1,0:T(8,128)(2,1)}) %reduce-scatter.2.cloned.1.call-update) | async-done | bytes 262160 | tf_op jit(solution)/shard_map/reduce_scatter | solution.py:145
  (18 shorter events, 0.2 us)
Async XLA Ops:
  6.5 164.1 %all-gather.2.cloned.1.call-start = ((), (), s32[]{:S(2)}) async-start(), calls=%async_computation.1 | async-start | bytes 6389760 | tf_op jit(solution)/shard_map/all_gather | solution.py:141
  8.1 19.6 %copy-start = (bf16[256,128]{1,0:T(8,128)(2,1)S(1)}, bf16[256,128]{1,0:T(8,128)(2,1)}, u32[]{:S(2)}) copy-start(bf16[256,128]{1,0:T(8,128)(2,1)} %param.11) | copy-start | bytes 196612
  8.1 215.8 %reduce-scatter.2.cloned.1.call-start = ((), (), s32[]{:S(2)}) async-start(), calls=%async_computation.2 | async-start | bytes 2359296 | tf_op jit(solution)/shard_map/reduce_scatter | solution.py:145
  8.1 19.5 %collective-permute-start = (bf16[256,128]{1,0:T(8,128)(2,1)}, bf16[256,128]{1,0:T(8,128)(2,1)S(1)}, u32[]{:S(2)}, u32[]{:S(2)}) collective-permute-start(bf16[256,128]{1,0:T(8,128)(2,1)} %param.11), channel_id=1, source_target_pairs={{0,16},{8,24},{16,32},{24,40},{32,48},{40,56},{48,64},{56,72},{64,... | collective-permute-start | bytes 196616 | tf_op jit(solution)/shard_map/ppermute | solution.py:13
  11.9 15.7 %collective-permute-start.1 = (bf16[256,128]{1,0:T(8,128)(2,1)}, bf16[256,128]{1,0:T(8,128)(2,1)S(1)}, u32[]{:S(2)}, u32[]{:S(2)}) collective-permute-start(bf16[256,128]{1,0:T(8,128)(2,1)} %param.11), channel_id=1, source_target_pairs={{0,8},{8,16},{16,24},{24,32},{32,40},{40,48},{48,56},{56,64},{64,7... | collective-permute-start | bytes 196616 | tf_op jit(solution)/shard_map/ppermute | solution.py:13
  13.8 14.6 %collective-permute-start.2 = (bf16[256,128]{1,0:T(8,128)(2,1)}, bf16[256,128]{1,0:T(8,128)(2,1)S(1)}, u32[]{:S(2)}, u32[]{:S(2)}) collective-permute-start(bf16[256,128]{1,0:T(8,128)(2,1)} %param.12), channel_id=1, source_target_pairs={{0,16},{8,24},{16,32},{24,40},{32,48},{40,56},{48,64},{56,72},{64,... | collective-permute-start | bytes 196616 | tf_op jit(solution)/shard_map/ppermute | solution.py:13
  18.8 9.6 %collective-permute-start.3 = (bf16[256,128]{1,0:T(8,128)(2,1)}, bf16[256,128]{1,0:T(8,128)(2,1)S(1)}, u32[]{:S(2)}, u32[]{:S(2)}) collective-permute-start(bf16[256,128]{1,0:T(8,128)(2,1)} %param.12), channel_id=1, source_target_pairs={{0,8},{8,16},{16,24},{24,32},{32,40},{40,48},{48,56},{56,64},{64,7... | collective-permute-start | bytes 196616 | tf_op jit(solution)/shard_map/ppermute | solution.py:13
  26.8 1.6 copy-start.1
  27.6 1.6 copy-start.2
  34.3 13.9 %collective-permute-start.4 = (f32[2,128,128]{2,0,1:T(2,128)S(1)}, f32[2,128,128]{2,0,1:T(2,128)S(1)}, u32[]{:S(2)}, u32[]{:S(2)}) collective-permute-start(f32[2,128,128]{2,0,1:T(2,128)S(1)} %get-tuple-element.7), channel_id=1, source_target_pairs={{8,0},{16,8},{24,16},{32,24},{40,32},{48,40},{56,48},{64,56},{72,6... | collective-permute-start | bytes 393224 | tf_op jit(solution)/shard_map/ppermute | solution.py:13
  37.8 10.4 %collective-permute-start.5 = (f32[2,128,128]{2,0,1:T(2,128)S(1)}, f32[2,128,128]{2,0,1:T(2,128)S(1)}, u32[]{:S(2)}, u32[]{:S(2)}) collective-permute-start(f32[2,128,128]{2,0,1:T(2,128)S(1)} %get-tuple-element.8), channel_id=1, source_target_pairs={{16,0},{24,8},{32,16},{40,24},{48,32},{56,40},{64,48},{72,56},{80,... | collective-permute-start | bytes 393224 | tf_op jit(solution)/shard_map/ppermute | solution.py:13
  44.0 4.4 %collective-permute-start.6 = (f32[2,128,128]{2,0,1:T(2,128)S(1)}, f32[2,128,128]{2,0,1:T(2,128)S(1)}, u32[]{:S(2)}, u32[]{:S(2)}) collective-permute-start(f32[2,128,128]{2,0,1:T(2,128)S(1)} %get-tuple-element.9), channel_id=1, source_target_pairs={{8,0},{16,8},{24,16},{32,24},{40,32},{48,40},{56,48},{64,56},{72,6... | collective-permute-start | bytes 393224 | tf_op jit(solution)/shard_map/ppermute | solution.py:13
  46.0 11.1 %collective-permute-start.7 = (f32[2,128,128]{2,0,1:T(2,128)S(1)}, f32[2,128,128]{2,0,1:T(2,128)S(1)}, u32[]{:S(2)}, u32[]{:S(2)}) collective-permute-start(f32[2,128,128]{2,0,1:T(2,128)S(1)} %get-tuple-element.10), channel_id=1, source_target_pairs={{16,0},{24,8},{32,16},{40,24},{48,32},{56,40},{64,48},{72,56},{80,... | collective-permute-start | bytes 393224 | tf_op jit(solution)/shard_map/ppermute | solution.py:13
Sparse Core Ops, SparseCore 0:
  10.6 159.9 all-gather.1
  176.7 47.1 reduce-scatter.1
where the time goes:
time: 231 us
  waiting for transfers between devices  169 us (73%)
  starting transfers between devices  23.5 us (10%)
  matrix products  15.1 us (7%)
  between operations  13.7 us (6%)
  local copies, waits for them, and re-layouts  4.78 us (2%)
  other arithmetic  4.14 us (2%)
    all_gather x1, waiting for transfers between devices, per_device(): lax.all_gather(weight_cat, 'ctx', axis=0, tiled=True)  113 us
    reduce_scatter x1, waiting for transfers between devices, per_device(): lax.psum_scatter(partial_value.astype(jnp.bfloat16), 'head', scatter_dime...  47.3 us
    ppermute x8, starting transfers between devices, passed_along(): return lax.ppermute(x, axis, pairs)  23.5 us
    ppermute x8, waiting for transfers between devices, passed_along(): return lax.ppermute(x, axis, pairs)  8.79 us
    dot_general x1, matrix products, per_device(): lax.dot_general(grads, lax.all_gather(weight_cat, 'ctx', axis=0, tiled=Tr...  5.96 us
  transfers between devices with their start and end apart: 10, of which 4 were waited for; matrix products, arithmetic and copies ran while one was open for 7% of the time, Pallas kernels for 0%

commit v1 on v0

--- a/solution.py
+++ b/solution.py
@@ -5,6 +5,13 @@
 from jax.sharding import PartitionSpec as P
 
 BLK = 128
+
+
+def swapped_in(block, axis, along):
+    devices = lax.axis_size(axis)
+    blocks = jnp.stack([block for _ in range(devices)])
+    blocks = lax.all_to_all(blocks, axis, split_axis=0, concat_axis=0)
+    return jnp.concatenate(blocks, axis=along)
 
 
 def passed_along(x, axis, by):
@@ -138,7 +145,7 @@
     weight_cat = jnp.concatenate([query_weight, key_weight, value_weight], axis=1)
     partial_value = lax.dot_general(
         grads,
-        lax.all_gather(weight_cat, "ctx", axis=0, tiled=True),
+        swapped_in(weight_cat, "ctx", 0),
         (((1,), (1,)), ((), ())),
         preferred_element_type=jnp.float32,
     )

time: 231 us -> 401 us (1.74)
  waiting for transfers between devices: 169 us -> 316 us
  starting transfers between devices: 23.5 us -> 40 us
    ppermute x8, waiting for transfers between devices: 8.79 us -> 258 us  [passed_along(): return lax.ppermute(x, axis, pairs)]
    all_gather x1 -> x0, waiting for transfers between devices: 113 us -> none  [per_device(): lax.all_gather(weight_cat, 'ctx', axis=0, tiled=True)]
    all_to_all x0 -> x1, starting transfers between devices: none -> 18.9 us  [swapped_in(): blocks = lax.all_to_all(blocks, axis, split_axis=0, concat_axis=0)]
    reduce_scatter x1, waiting for transfers between devices: 47.3 us -> 57.7 us  [per_device(): lax.psum_scatter(partial_value.astype(jnp.bfloat16), 'head', scatter_dime...]
  transfers between devices with their start and end apart: 10 -> 10, of which waited for: 4 -> 3; matrix products, arithmetic and copies ran while one was open for 7% -> 5% of each run, Pallas kernels for 0% -> 0%
where the time goes in v1:
time: 401 us; the launch traced here: 400 us
  waiting for transfers between devices  316 us (79%)
  starting transfers between devices  40 us (10%)
  matrix products  17.3 us (4%)
  between operations  13.8 us (3%)
  local copies, waits for them, and re-layouts  8.38 us (2%)
  other arithmetic  4.37 us (1%)
    ppermute x8, waiting for transfers between devices, passed_along(): return lax.ppermute(x, axis, pairs)  258 us
    reduce_scatter x1, waiting for transfers between devices, per_device(): lax.psum_scatter(partial_value.astype(jnp.bfloat16), 'head', scatter_dime...  57.7 us
    ppermute x8, starting transfers between devices, passed_along(): return lax.ppermute(x, axis, pairs)  21 us
    all_to_all x1, starting transfers between devices, swapped_in(): blocks = lax.all_to_all(blocks, axis, split_axis=0, concat_axis=0)  18.9 us
  transfers between devices with their start and end apart: 10, of which 3 were waited for; matrix products, arithmetic and copies ran while one was open for 5% of the time, Pallas kernels for 0%

profile of v1, /device:TPU:4, one launch (start us, length us, event | category | flops | bytes accessed | tf_op | source)
XLA Modules:
  0.0 400.0 jit_solution(10323380798773277134)
XLA Ops:
  6.5 0.9 pad_maximum_fusion.2
  7.4 3.4 stack.2
  10.8 0.0 copy-start.4
  10.8 0.0 copy-start.7
  10.8 18.9 %all-to-all-start = ((bf16[64,64,768]{2,1,0:T(8,128)(2,1)}), bf16[64,64,768]{2,1,0:T(8,128)(2,1)}, u32[]{:S(2)}, u32[]{:S(2)}) async-start(bf16[64,64,768]{2,1,0:T(8,128)(2,1)} %stack.2), calls=%async_computation | async-start | bytes 12582912 | tf_op jit(solution)/shard_map/all_to_all | solution.py:13
  29.8 0.0 reduce-scatter.2.cloned.1.call-start
  29.8 2.0 collective-permute-start.1
  31.8 3.4 collective-permute-start
  35.2 4.6 %collective-permute-start.3 = (bf16[256,128]{1,0:T(8,128)(2,1)S(1)}, bf16[256,128]{1,0:T(8,128)(2,1)}, u32[]{:S(2)}, u32[]{:S(2)}) collective-permute-start(bf16[256,128]{1,0:T(8,128)(2,1)S(1)} %copy-done.9), channel_id=1, source_target_pairs={{0,8},{8,16},{16,24},{24,32},{32,40},{40,48},{48,56},{56,64},{64,7... | collective-permute-start | bytes 196616 | tf_op jit(solution)/shard_map/ppermute | solution.py:20
  39.8 3.4 collective-permute-start.2
  43.3 0.1 compare_select_fusion
  43.3 0.1 copy.38
  43.4 0.1 reshape.60
  43.5 0.1 compare_and_fusion
  43.6 0.7 copy.41
  44.3 0.1 copy.40
  44.4 0.8 reshape.52
  45.2 0.1 reshape.55
  45.3 0.1 copy.50
  45.4 0.1 convert_multiply_fusion
  45.4 0.2 reshape.56
  45.6 0.3 reduce_sum.9
  46.0 0.1 copy.46
  46.1 0.6 iota_compare_fusion
  46.7 252.0 %collective-permute-done = bf16[256,128]{1,0:T(8,128)(2,1)S(1)} collective-permute-done((bf16[256,128]{1,0:T(8,128)(2,1)S(1)}, bf16[256,128]{1,0:T(8,128)(2,1)S(1)}, u32[]{:S(2)}, u32[]{:S(2)}) %collective-permute-start) | collective-permute-done | bytes 65568 | tf_op jit(solution)/shard_map/ppermute | solution.py:20
  298.7 0.7 gather_fusion
  299.5 1.9 bitcast_select_fusion
  301.5 0.4 fusion.14
  301.9 3.3 fusion.8
  305.2 0.9 fusion.35
  306.1 1.9 collective-permute-start.7
  308.0 1.9 collective-permute-start.6
  310.0 0.9 pad_maximum_fusion.1
  310.9 0.7 gather_fusion.1
  311.6 1.4 fusion
  313.1 0.4 convolution_multiply_fusion
  313.5 3.3 fusion.5
  316.8 0.5 fusion.13
  317.3 0.1 fusion.34
  317.4 1.9 collective-permute-start.5
  319.3 1.9 collective-permute-start.4
  321.2 0.2 copy.48
  321.5 1.2 fusion.26
  322.8 6.4 %collective-permute-done.5 = f32[2,128,128]{2,0,1:T(2,128)S(1)} collective-permute-done((f32[2,128,128]{2,0,1:T(2,128)S(1)}, f32[2,128,128]{2,0,1:T(2,128)S(1)}, u32[]{:S(2)}, u32[]{:S(2)}) %collective-permute-start.5) | collective-permute-done | bytes 131104 | tf_op jit(solution)/shard_map/ppermute | solution.py:20
  329.2 0.1 fusion.28
  329.4 6.0 %convolution_convert_fusion = bf16[256,4096]{1,0:T(8,128)(2,1)} fusion(bf16[4096,768]{1,0:T(8,128)(2,1)} %bitcast.28, bf16[256,128]{1,0:T(8,128)(2,1)S(1)} %bitcast.71, bf16[256,128]{1,0:T(8,128)(2,1)S(1)} %bitcast.72, bf16[256,512]{1,0:T(8,128)(2,1)S(1)} %bitcast.70), kind=kOutput, calls=%fused_computation.2 | convolution fusion | flops 1612840960 | bytes 8781824 | tf_op jit(solution)/shard_map/dot_general | solution.py:146
  335.4 0.0 reduce-scatter.2.cloned.1.call-update
  335.4 57.7 %reduce-scatter.2.cloned.1.call-done = bf16[256,512]{1,0:T(8,128)(2,1)} async-done(((bf16[256,4096]{1,0:T(8,128)(2,1)}), bf16[256,512]{1,0:T(8,128)(2,1)}) %reduce-scatter.2.cloned.1.call-update) | async-done | bytes 262160 | tf_op jit(solution)/shard_map/reduce_scatter | solution.py:152
  (36 shorter events, 0.2 us)
Async XLA Ops:
  10.8 19.0 %copy-start.8 = (bf16[256,128]{1,0:T(8,128)(2,1)S(1)}, bf16[256,128]{1,0:T(8,128)(2,1)}, u32[]{:S(2)}) copy-start(bf16[256,128]{1,0:T(8,128)(2,1)} %param.11) | copy-start | bytes 196612
  10.8 24.4 %copy-start.9 = (bf16[256,128]{1,0:T(8,128)(2,1)S(1)}, bf16[256,128]{1,0:T(8,128)(2,1)}, u32[]{:S(2)}) copy-start(bf16[256,128]{1,0:T(8,128)(2,1)} %param.12) | copy-start | bytes 196612
  10.8 32.4 %copy-start.11 = (s32[2,4,3]{1,0,2:T(2,128)S(1)}, s32[2,4,3]{1,0,2:T(2,128)}, u32[]{:S(2)}) copy-start(s32[2,4,3]{1,0,2:T(2,128)} %param.16) | copy-start | bytes 292
  10.8 33.6 %copy-start.6 = (bf16[256,512]{1,0:T(8,128)(2,1)S(1)}, bf16[256,512]{1,0:T(8,128)(2,1)}, u32[]{:S(2)}) copy-start(bf16[256,512]{1,0:T(8,128)(2,1)} %param.10) | copy-start | bytes 786436
  10.8 34.4 %copy-start.4 = (bf16[256,512]{1,0:T(8,128)(2,1)S(1)}, bf16[256,512]{1,0:T(8,128)(2,1)}, u32[]{:S(2)}) copy-start(bf16[256,512]{1,0:T(8,128)(2,1)} %param.14) | copy-start | bytes 786436
  10.8 34.6 %copy-start.7 = (bf16[256,512]{1,0:T(8,128)(2,1)S(1)}, bf16[256,512]{1,0:T(8,128)(2,1)}, u32[]{:S(2)}) copy-start(bf16[256,512]{1,0:T(8,128)(2,1)} %param.13) | copy-start | bytes 786436
  10.8 318.6 %all-to-all-start = ((bf16[64,64,768]{2,1,0:T(8,128)(2,1)}), bf16[64,64,768]{2,1,0:T(8,128)(2,1)}, u32[]{:S(2)}, u32[]{:S(2)}) async-start(bf16[64,64,768]{2,1,0:T(8,128)(2,1)} %stack.2), calls=%async_computation | async-start | bytes 12582912 | tf_op jit(solution)/shard_map/all_to_all | solution.py:13
  29.8 363.4 %reduce-scatter.2.cloned.1.call-start = ((), (), s32[]{:S(2)}) async-start(), calls=%async_computation.2 | async-start | bytes 2359296 | tf_op jit(solution)/shard_map/reduce_scatter | solution.py:152
  29.8 16.9 %collective-permute-start.1 = (bf16[256,128]{1,0:T(8,128)(2,1)S(1)}, bf16[256,128]{1,0:T(8,128)(2,1)S(1)}, u32[]{:S(2)}, u32[]{:S(2)}) collective-permute-start(bf16[256,128]{1,0:T(8,128)(2,1)S(1)} %copy-done.8), channel_id=1, source_target_pairs={{0,8},{8,16},{16,24},{24,32},{32,40},{40,48},{48,56},{56,64},{64,7... | collective-permute-start | bytes 196616 | tf_op jit(solution)/shard_map/ppermute | solution.py:20
  31.8 266.8 %collective-permute-start = (bf16[256,128]{1,0:T(8,128)(2,1)S(1)}, bf16[256,128]{1,0:T(8,128)(2,1)S(1)}, u32[]{:S(2)}, u32[]{:S(2)}) collective-permute-start(bf16[256,128]{1,0:T(8,128)(2,1)S(1)} %copy-done.8), channel_id=1, source_target_pairs={{0,16},{8,24},{16,32},{24,40},{32,48},{40,56},{48,64},{56,72},{64,... | collective-permute-start | bytes 196616 | tf_op jit(solution)/shard_map/ppermute | solution.py:20
  35.2 274.7 %collective-permute-start.3 = (bf16[256,128]{1,0:T(8,128)(2,1)S(1)}, bf16[256,128]{1,0:T(8,128)(2,1)}, u32[]{:S(2)}, u32[]{:S(2)}) collective-permute-start(bf16[256,128]{1,0:T(8,128)(2,1)S(1)} %copy-done.9), channel_id=1, source_target_pairs={{0,8},{8,16},{16,24},{24,32},{32,40},{40,48},{48,56},{56,64},{64,7... | collective-permute-start | bytes 196616 | tf_op jit(solution)/shard_map/ppermute | solution.py:20
  39.8 270.1 %collective-permute-start.2 = (bf16[256,128]{1,0:T(8,128)(2,1)S(1)}, bf16[256,128]{1,0:T(8,128)(2,1)}, u32[]{:S(2)}, u32[]{:S(2)}) collective-permute-start(bf16[256,128]{1,0:T(8,128)(2,1)S(1)} %copy-done.9), channel_id=1, source_target_pairs={{0,16},{8,24},{16,32},{24,40},{32,48},{40,56},{48,64},{56,72},{64,... | collective-permute-start | bytes 196616 | tf_op jit(solution)/shard_map/ppermute | solution.py:20
  45.3 256.2 %copy-start.2 = (bf16[2,128,4,128]{3,2,1,0:T(4,128)(2,1)}, bf16[2,128,4,128]{3,2,1,0:T(4,128)(2,1)S(1)}, u32[]{:S(2)}) copy-start(bf16[2,128,4,128]{3,2,1,0:T(4,128)(2,1)S(1)} %reshape.55) | copy-start | bytes 786436
  298.7 0.8 copy-start.10
  299.5 2.0 copy-start
  305.2 5.7 %copy-start.3 = (f32[6,128,128]{2,0,1:T(8,128)}, f32[6,128,128]{2,0,1:T(8,128)S(1)}, u32[]{:S(2)}) copy-start(f32[6,128,128]{2,0,1:T(8,128)S(1)} %fusion.8) | copy-start | bytes 1179652
  306.1 15.4 %collective-permute-start.7 = (f32[2,128,128]{2,0,1:T(2,128)}, f32[2,128,128]{2,0,1:T(2,128)S(1)}, u32[]{:S(2)}, u32[]{:S(2)}) collective-permute-start(f32[2,128,128]{2,0,1:T(2,128)} %get-tuple-element.10), channel_id=1, source_target_pairs={{16,0},{24,8},{32,16},{40,24},{48,32},{56,40},{64,48},{72,56},{80,... | collective-permute-start | bytes 393224 | tf_op jit(solution)/shard_map/ppermute | solution.py:20
  308.0 13.5 %collective-permute-start.6 = (f32[2,128,128]{2,0,1:T(2,128)}, f32[2,128,128]{2,0,1:T(2,128)}, u32[]{:S(2)}, u32[]{:S(2)}) collective-permute-start(f32[2,128,128]{2,0,1:T(2,128)} %get-tuple-element.9), channel_id=1, source_target_pairs={{8,0},{16,8},{24,16},{32,24},{40,32},{48,40},{56,48},{64,56},{72,6... | collective-permute-start | bytes 393224 | tf_op jit(solution)/shard_map/ppermute | solution.py:20
  311.6 1.4 copy-start.5
  313.5 3.3 copy-start.1
  317.4 11.8 %collective-permute-start.5 = (f32[2,128,128]{2,0,1:T(2,128)S(1)}, f32[2,128,128]{2,0,1:T(2,128)S(1)}, u32[]{:S(2)}, u32[]{:S(2)}) collective-permute-start(f32[2,128,128]{2,0,1:T(2,128)S(1)} %get-tuple-element.8), channel_id=1, source_target_pairs={{16,0},{24,8},{32,16},{40,24},{48,32},{56,40},{64,48},{72,56},{80,... | collective-permute-start | bytes 393224 | tf_op jit(solution)/shard_map/ppermute | solution.py:20
  319.3 9.9 %collective-permute-start.4 = (f32[2,128,128]{2,0,1:T(2,128)S(1)}, f32[2,128,128]{2,0,1:T(2,128)S(1)}, u32[]{:S(2)}, u32[]{:S(2)}) collective-permute-start(f32[2,128,128]{2,0,1:T(2,128)S(1)} %get-tuple-element.7), channel_id=1, source_target_pairs={{8,0},{16,8},{24,16},{32,24},{40,32},{48,40},{56,48},{64,56},{72,6... | collective-permute-start | bytes 393224 | tf_op jit(solution)/shard_map/ppermute | solution.py:20
Sparse Core Ops, SparseCore 0:
  335.5 57.5 reduce-scatter.1
